TPU v7x, 256 devices: a whole 4x4x8 slice. The times are simulated.
256 devices in a mesh: prop: 8 (over x, core), dom: 32 (over z, y).
Axes of the slice: x: 4, y: 4, z: 8, core: 2. Of those that a mesh axis runs over, the one named last changes fastest.
Arguments:
- states: float32 [8, 128, 64, 128], P('prop', 'dom'), may hold values from -4 to 4
- accepted: int32 [1], replicated, may hold values from 0 to 7
- noise: float32 [8, 128, 64, 128], P('prop', 'dom'), may hold values from -5 to 5
- source: float32 [128, 64, 128], P('dom'), may hold values from -6 to 6
Outputs:
- pressure: float32 [8, 128, 64, 128], P('prop', 'dom')
All inputs are finite; a program needn't handle non-finite values.
Results may differ from a plain program's by a relative error of at most 0.0003.
Values sent between devices are 32-bit elements; how exact they have to be, the bound alone decides.
A program may use at most 128 MiB of HBM per device.

v0:
```python
import math
import jax
import jax.numpy as jnp
from jax import lax
from jax.sharding import PartitionSpec as P

LEVELS = 4
SWEEPS = 2
COARSE_SWEEPS = 64
OMEGA = 0.7
BETA = 0.4
SHRINK = math.sqrt(1.0 - BETA * BETA)
ZSCALE = 16.0


def padded_2(x, sides, width):
    for axis, dim in sides:
        devices, length = (lax.axis_size(axis), x.shape[dim])
        up = [(i, (i + 1) % devices) for i in range(devices - 1)]
        down = [(j, i) for i, j in up]
        last = lax.slice_in_dim(x, length - width, length, axis=dim)
        initial = lax.slice_in_dim(x, 0, width, axis=dim)
        before = lax.ppermute(last, axis, up)
        after = lax.ppermute(initial, axis, down)
        x = jnp.concatenate([before, x, after], axis=dim)
    return x


def from_root(x, axis, root):
    mine = lax.axis_index(axis) == root
    return lax.psum(jnp.where(mine, x, jnp.zeros_like(x)), axis)


def shift_lower(values, axis):
    axis = values.ndim + axis
    count = values.shape[axis]
    kept = lax.slice_in_dim(values, 0, count - 1, axis=axis)
    return jnp.concatenate(
        [jnp.zeros_like(lax.slice_in_dim(values, 0, 1, axis=axis)), kept], axis=axis
    )


def shift_upper(values, axis):
    axis = values.ndim + axis
    count = values.shape[axis]
    kept = lax.slice_in_dim(values, 1, count, axis=axis)
    return jnp.concatenate(
        [kept, jnp.zeros_like(lax.slice_in_dim(values, 0, 1, axis=axis))], axis=axis
    )


def harmonic(first, second):
    return 2.0 * first * second / (first + second)


def coefficients(perm, padded, scale):
    inner_x = harmonic(perm[..., 1:, :], perm[..., :-1, :])
    west = jnp.concatenate([perm[..., :1, :], inner_x], axis=-2)
    east = jnp.concatenate([inner_x, perm[..., -1:, :]], axis=-2)
    inner_y = harmonic(perm[..., 1:], perm[..., :-1])
    south = jnp.concatenate([perm[..., :1], inner_y], axis=-1)
    north = jnp.concatenate([inner_y, perm[..., -1:]], axis=-1)
    below = harmonic(padded[..., :-2, :, :], perm)
    above = harmonic(padded[..., 2:, :, :], perm)
    zfactor = ZSCALE * scale
    parts = [
        west * scale,
        east * scale,
        south * scale,
        north * scale,
        below * zfactor,
        above * zfactor,
    ]
    diagonal = parts[0] + parts[1] + parts[2] + parts[3] + parts[4] + parts[5]
    return parts + [diagonal, OMEGA / diagonal]


def apply_op(values, padded, coefs):
    result = (
        coefs[6] * values - coefs[0] * shift_lower(values, -2) - coefs[1] * shift_upper(values, -2)
    )
    result = result - coefs[2] * shift_lower(values, -1) - coefs[3] * shift_upper(values, -1)
    return result - coefs[4] * padded[..., :-2, :, :] - coefs[5] * padded[..., 2:, :, :]


def sweep(values, right, coefs, pad_z):
    return values + coefs[7] * (right - apply_op(values, pad_z(values), coefs))


def sum_children(values):
    shape = values.shape
    split = values.reshape(shape[:-3] + (shape[-3] // 2, 2, shape[-2] // 2, 2, shape[-1] // 2, 2))
    return split.sum(axis=(-5, -3, -1))


def prolong(values):
    return jnp.repeat(jnp.repeat(jnp.repeat(values, 2, axis=-3), 2, axis=-2), 2, axis=-1)


def zero_pad(values):
    widths = [(0, 0)] * (values.ndim - 3) + [(1, 1), (0, 0), (0, 0)]
    return jnp.pad(values, widths)


def pressure_rim(values):
    return padded_2(values, (("dom", 1),), 1)


def perm_rim(values):
    return padded_2(values, (("dom", 1),), 1)


def coarse_solve(right, perm, level, pad_z, pad_perm):
    coefs = coefficients(perm, pad_perm(perm), 4.0**level)
    start = coefs[7] * right
    return lax.fori_loop(
        0, COARSE_SWEEPS - 1, lambda step, values: sweep(values, right, coefs, pad_z), start
    )


def level_cycle(right, perm, level, pad_z, pad_perm, deeper):
    coefs = coefficients(perm, pad_perm(perm), 4.0**level)
    values = coefs[7] * right
    values = sweep(values, right, coefs, pad_z)
    residue = right - apply_op(values, pad_z(values), coefs)
    update = deeper(sum_children(residue), sum_children(perm) * 0.125, level + 1)
    values = values + prolong(update)
    for step in range(SWEEPS):
        values = sweep(values, right, coefs, pad_z)
    return values


def local_cycle(right, perm, level):
    if level == LEVELS - 1:
        return coarse_solve(right, perm, level, zero_pad, zero_pad)
    return level_cycle(right, perm, level, zero_pad, zero_pad, local_cycle)


def body(states, accepted, noise, source):
    per_device = states.shape[0]
    chosen = accepted[0]
    owner = chosen // per_device
    picked = lax.dynamic_index_in_dim(states, chosen % per_device, 0, keepdims=False)
    current = from_root(picked, "prop", owner)
    theta = SHRINK * current[None] + BETA * noise
    perm = jnp.exp(theta)
    right = source[None]
    gather_level = 2

    def spread_cycle(right_side, field, level):
        if level == gather_level:
            whole_right, whole_perm = (
                lax.all_gather(right_side, "dom", axis=1, tiled=True),
                lax.all_gather(field, "dom", axis=1, tiled=True),
            )
            result = local_cycle(whole_right, whole_perm, level)
            height = right_side.shape[1]
            return lax.dynamic_slice_in_dim(result, lax.axis_index("dom") * height, height, 1)
        return level_cycle(right_side, field, level, pressure_rim, perm_rim, spread_cycle)

    return spread_cycle(right, perm, 0)


def solution(mesh):
    in_specs = (
        P("prop", "dom", None, None),
        P(),
        P("prop", "dom", None, None),
        P("dom", None, None),
    )
    out_specs = P("prop", "dom", None, None)
    return jax.shard_map(body, mesh=mesh, in_specs=in_specs, out_specs=out_specs, check_vma=False)
```

profile of v0, /device:TPU:120, one launch (start us, length us, event | category | flops | bytes accessed | tf_op | source)
XLA Modules:
  0.0 459.8 jit_solution(12875724920466572557)
XLA Ops:
  11.1 65.1 %all-reduce.61.cloned.1.call-done = f32[4,64,128]{1,2,0:T(8,128)} async-done(((f32[4,64,128]{1,2,0:T(8,128)}), f32[4,64,128]{1,2,0:T(8,128)}) %all-reduce.61.cloned.1.call-update) | async-done | bytes 131088 | tf_op jit(solution)/shard_map/psum | solution.py:31
  78.3 9.8 %reshape.767 = f32[2,2,32,2,64,2]{5,4,3,2,1,0:T(8,128)} reshape(f32[1,4,64,128]{3,2,1,0:T(8,128)S(1)} %copy.50) | data formatting | bytes 262144 | tf_op jit(solution)/shard_map/reshape | solution.py:92
  88.1 4.0 reduce_sum.74
  94.8 48.6 %all-gather = f32[512,32]{1,0:T(8,128)S(1)} all-gather(f32[16,32]{1,0:T(8,128)S(1)} %broadcast_multiply_fusion), channel_id=2, replica_groups=mesh['prop'=8,'dom'=32] {'dom'}, dimensions={0}, use_global_device_ids=true | all-gather | bytes 67584 | tf_op jit(solution)/shard_map/all_gather | solution.py:154
  145.8 5.5 %reshape.769 = f32[16,2,8,2,16,2]{3,2,1,0,5,4:T(8,128)} reshape(f32[512,32]{0,1:T(8,128)S(1)} %copy.52) | data formatting | bytes 131072 | tf_op jit(solution)/shard_map/reshape | solution.py:92
  151.4 2.6 reduce_sum.84
  154.2 4.6 collective-permute-start
  160.8 7.2 %collective-permute-start.4 = (f32[1,1,32,64]{3,2,1,0:T(8,128)}, f32[1,1,32,64]{3,2,1,0:T(8,128)S(1)}, u32[]{:S(2)}, u32[]{:S(2)}) collective-permute-start(f32[1,1,32,64]{3,2,1,0:T(8,128)} %get-tuple-element.298), channel_id=1, source_target_pairs={{0,1},{1,2},{2,3},{3,4},{4,5},{5,6},{6,7},{7,8},{8,9},{9,10},{10,1... | collective-permute-start | bytes 24584 | tf_op jit(solution)/shard_map/ppermute | solution.py:23
  179.0 7.2 %collective-permute-start.2 = (f32[1,1,64,128]{2,3,1,0:T(8,128)S(1)}, f32[1,1,64,128]{2,3,1,0:T(8,128)S(1)}, u32[]{:S(2)}, u32[]{:S(2)}) collective-permute-start(f32[1,1,64,128]{2,3,1,0:T(8,128)S(1)} %get-tuple-element.255), channel_id=1, source_target_pairs={{0,1},{1,2},{2,3},{3,4},{4,5},{5,6},{6,7},{7,8},{8,9},{9,10},{10,1... | collective-permute-start | bytes 98312 | tf_op jit(solution)/shard_map/ppermute | solution.py:23
  186.2 1.9 collective-permute-start.3
  188.2 7.5 %collective-permute-done.3 = f32[1,1,64,128]{2,3,1,0:T(8,128)S(1)} collective-permute-done((f32[1,1,64,128]{2,3,1,0:T(8,128)S(1)}, f32[1,1,64,128]{2,3,1,0:T(8,128)S(1)}, u32[]{:S(2)}, u32[]{:S(2)}) %collective-permute-start.3) | collective-permute-done | bytes 32800 | tf_op jit(solution)/shard_map/ppermute | solution.py:24
  198.2 3.9 collective-permute-start.7
  202.4 5.2 %collective-permute-done.7 = f32[1,1,64,128]{2,3,1,0:T(8,128)S(1)} collective-permute-done((f32[1,1,64,128]{2,3,1,0:T(8,128)S(1)}, f32[1,1,64,128]{2,3,1,0:T(8,128)S(1)}, u32[]{:S(2)}, u32[]{:S(2)}) %collective-permute-start.7) | collective-permute-done | bytes 32800 | tf_op jit(solution)/shard_map/ppermute | solution.py:24
  208.2 9.8 %reshape.768 = f32[2,2,32,2,64,2]{5,4,3,2,1,0:T(8,128)} reshape(f32[1,4,64,128]{3,2,1,0:T(8,128)S(1)} %copy.51) | data formatting | bytes 262144 | tf_op jit(solution)/shard_map/reshape | solution.py:92
  218.0 4.0 reduce_sum.75
  224.2 3.9 collective-permute-start.9
  228.2 4.9 %collective-permute-done.9 = f32[1,1,32,64]{3,2,1,0:T(8,128)S(1)} collective-permute-done((f32[1,1,32,64]{3,2,1,0:T(8,128)S(1)}, f32[1,1,32,64]{3,2,1,0:T(8,128)S(1)}, u32[]{:S(2)}, u32[]{:S(2)}) %collective-permute-start.9) | collective-permute-done | bytes 8224 | tf_op jit(solution)/shard_map/ppermute | solution.py:24
  235.2 3.9 collective-permute-start.11
  239.2 4.9 %collective-permute-done.11 = f32[1,1,32,64]{3,2,1,0:T(8,128)S(1)} collective-permute-done((f32[1,1,32,64]{3,2,1,0:T(8,128)S(1)}, f32[1,1,32,64]{3,2,1,0:T(8,128)S(1)}, u32[]{:S(2)}, u32[]{:S(2)}) %collective-permute-start.11) | collective-permute-done | bytes 8224 | tf_op jit(solution)/shard_map/ppermute | solution.py:24
  245.0 46.0 %all-gather.1 = f32[512,32]{1,0:T(8,128)S(1)} all-gather(f32[16,32]{1,0:T(8,128)S(1)} %reduce_sum.82), channel_id=3, replica_groups=mesh['prop'=8,'dom'=32] {'dom'}, dimensions={0}, use_global_device_ids=true | all-gather | bytes 67584 | tf_op jit(solution)/shard_map/all_gather | solution.py:153
  295.8 4.5 reshape.770
  300.3 2.5 reduce_sum.85
  307.9 84.0 %while.15 = (s32[]{:T(128)}, f32[1,16,8,16]{3,2,1,0:T(8,128)S(1)}, f32[1,16,8,16]{3,2,1,0:T(8,128)}, f32[1,16,8,16]{3,2,1,0:T(8,128)}, f32[1,16,8,16]{3,2,1,0:T(...) while((s32[]{:T(128)}, f32[1,16,8,16]{3,2,1,0:T(8,128)S(1)}, ...), condition=%wide.region_10.11_spmd, body=%wide.region_9.10_spmd.sunk | while | flops 32770 | bytes 195701 | solution.py:116
  400.2 4.6 collective-permute-start.12
  404.8 1.9 collective-permute-start.13
  406.8 7.0 %collective-permute-done.13 = f32[1,1,32,64]{3,2,1,0:T(8,128)S(1)} collective-permute-done((f32[1,1,32,64]{3,2,1,0:T(8,128)S(1)}, f32[1,1,32,64]{3,2,1,0:T(8,128)S(1)}, u32[]{:S(2)}, u32[]{:S(2)}) %collective-permute-start.13) | collective-permute-done | bytes 8224 | tf_op jit(solution)/shard_map/ppermute | solution.py:24
  416.7 3.9 collective-permute-start.15
  420.7 4.9 %collective-permute-done.15 = f32[1,1,32,64]{3,2,1,0:T(8,128)S(1)} collective-permute-done((f32[1,1,32,64]{3,2,1,0:T(8,128)S(1)}, f32[1,1,32,64]{3,2,1,0:T(8,128)S(1)}, u32[]{:S(2)}, u32[]{:S(2)}) %collective-permute-start.15) | collective-permute-done | bytes 8224 | tf_op jit(solution)/shard_map/ppermute | solution.py:24
  428.8 3.9 collective-permute-start.17
  433.1 5.2 %collective-permute-done.17 = f32[1,1,64,128]{2,3,1,0:T(8,128)S(1)} collective-permute-done((f32[1,1,64,128]{2,3,1,0:T(8,128)S(1)}, f32[1,1,64,128]{2,3,1,0:T(8,128)S(1)}, u32[]{:S(2)}, u32[]{:S(2)}) %collective-permute-start.17) | collective-permute-done | bytes 32800 | tf_op jit(solution)/shard_map/ppermute | solution.py:24
  441.5 3.9 collective-permute-start.19
  445.8 5.2 %collective-permute-done.19 = f32[1,1,64,128]{2,3,1,0:T(8,128)S(1)} collective-permute-done((f32[1,1,64,128]{2,3,1,0:T(8,128)S(1)}, f32[1,1,64,128]{2,3,1,0:T(8,128)S(1)}, u32[]{:S(2)}, u32[]{:S(2)}) %collective-permute-start.19) | collective-permute-done | bytes 32800 | tf_op jit(solution)/shard_map/ppermute | solution.py:24
  (429 shorter events, 144.2 us)
Async XLA Ops:
  6.5 69.6 %all-reduce.61.cloned.1.call-start = ((), (), s32[]{:S(2)}) async-start(), calls=%async_computation | async-start | bytes 524288 | tf_op jit(solution)/shard_map/psum | solution.py:31
  77.8 129.9 %copy-start.18 = (f32[1,4,64,1]{2,3,1,0:T(1,128)}, f32[1,4,64,1]{2,3,1,0:T(1,128)S(1)}, u32[]{:S(2)}) copy-start(f32[1,4,64,1]{2,3,1,0:T(1,128)S(1)} %get-tuple-element.261) | copy-start | bytes 3076
  77.8 129.9 %copy-start.19 = (f32[1,4,64,1]{2,3,1,0:T(1,128)}, f32[1,4,64,1]{2,3,1,0:T(1,128)S(1)}, u32[]{:S(2)}) copy-start(f32[1,4,64,1]{2,3,1,0:T(1,128)S(1)} %get-tuple-element.262) | copy-start | bytes 3076
  93.3 150.8 %copy-start.8 = (f32[1,2,31,64]{3,2,1,0:T(8,128)}, f32[1,2,31,64]{3,2,1,0:T(8,128)S(1)}, u32[]{:S(2)}) copy-start(f32[1,2,31,64]{3,2,1,0:T(8,128)S(1)} %add_divide_fusion.7) | copy-start | bytes 47620
  154.2 24.2 %collective-permute-start = (f32[1,1,64,128]{2,3,1,0:T(8,128)}, f32[1,1,64,128]{2,3,1,0:T(8,128)S(1)}, u32[]{:S(2)}, u32[]{:S(2)}) collective-permute-start(f32[1,1,64,128]{2,3,1,0:T(8,128)} %get-tuple-element.260), channel_id=1, source_target_pairs={{0,1},{1,2},{2,3},{3,4},{4,5},{5,6},{6,7},{7,8},{8,9},{9,10},{10,1... | collective-permute-start | bytes 98312 | tf_op jit(solution)/shard_map/ppermute | solution.py:23
  158.8 19.6 %collective-permute-start.1 = (f32[1,1,64,128]{2,3,1,0:T(8,128)}, f32[1,1,64,128]{2,3,1,0:T(8,128)S(1)}, u32[]{:S(2)}, u32[]{:S(2)}) collective-permute-start(f32[1,1,64,128]{2,3,1,0:T(8,128)} %get-tuple-element.259), channel_id=1, source_target_pairs={{1,0},{2,1},{3,2},{4,3},{5,4},{6,5},{7,6},{8,7},{9,8},{10,9},{11,1... | collective-permute-start | bytes 98312 | tf_op jit(solution)/shard_map/ppermute | solution.py:24
  160.8 61.3 %collective-permute-start.4 = (f32[1,1,32,64]{3,2,1,0:T(8,128)}, f32[1,1,32,64]{3,2,1,0:T(8,128)S(1)}, u32[]{:S(2)}, u32[]{:S(2)}) collective-permute-start(f32[1,1,32,64]{3,2,1,0:T(8,128)} %get-tuple-element.298), channel_id=1, source_target_pairs={{0,1},{1,2},{2,3},{3,4},{4,5},{5,6},{6,7},{7,8},{8,9},{9,10},{10,1... | collective-permute-start | bytes 24584 | tf_op jit(solution)/shard_map/ppermute | solution.py:23
  168.0 54.1 %collective-permute-start.5 = (f32[1,1,32,64]{3,2,1,0:T(8,128)}, f32[1,1,32,64]{3,2,1,0:T(8,128)S(1)}, u32[]{:S(2)}, u32[]{:S(2)}) collective-permute-start(f32[1,1,32,64]{3,2,1,0:T(8,128)} %get-tuple-element.297), channel_id=1, source_target_pairs={{1,0},{2,1},{3,2},{4,3},{5,4},{6,5},{7,6},{8,7},{9,8},{10,9},{11,1... | collective-permute-start | bytes 24584 | tf_op jit(solution)/shard_map/ppermute | solution.py:24
  170.8 24.9 %copy-start.7 = (f32[1,16,8,16]{2,1,3,0:T(8,128)}, f32[1,16,8,16]{2,1,3,0:T(8,128)S(1)}, u32[]{:S(2)}) copy-start(f32[1,16,8,16]{2,1,3,0:T(8,128)S(1)} %get-tuple-element.188) | copy-start | bytes 24580
  178.5 39.6 %copy-start.1 = (f32[1,1,64,128]{2,3,1,0:T(8,128)}, f32[1,1,64,128]{2,3,1,0:T(8,128)S(1)}, u32[]{:S(2)}) copy-start(f32[1,1,64,128]{2,3,1,0:T(8,128)S(1)} %collective-permute-done) | copy-start | bytes 98308
  178.5 39.6 %copy-start.3 = (f32[1,1,64,128]{2,3,1,0:T(8,128)}, f32[1,1,64,128]{2,3,1,0:T(8,128)S(1)}, u32[]{:S(2)}) copy-start(f32[1,1,64,128]{2,3,1,0:T(8,128)S(1)} %collective-permute-done.1) | copy-start | bytes 98308
  179.0 9.2 %collective-permute-start.2 = (f32[1,1,64,128]{2,3,1,0:T(8,128)S(1)}, f32[1,1,64,128]{2,3,1,0:T(8,128)S(1)}, u32[]{:S(2)}, u32[]{:S(2)}) collective-permute-start(f32[1,1,64,128]{2,3,1,0:T(8,128)S(1)} %get-tuple-element.255), channel_id=1, source_target_pairs={{0,1},{1,2},{2,3},{3,4},{4,5},{5,6},{6,7},{7,8},{8,9},{9,10},{10,1... | collective-permute-start | bytes 98312 | tf_op jit(solution)/shard_map/ppermute | solution.py:23
  186.2 9.5 %collective-permute-start.3 = (f32[1,1,64,128]{2,3,1,0:T(8,128)S(1)}, f32[1,1,64,128]{2,3,1,0:T(8,128)S(1)}, u32[]{:S(2)}, u32[]{:S(2)}) collective-permute-start(f32[1,1,64,128]{2,3,1,0:T(8,128)S(1)} %get-tuple-element.256), channel_id=1, source_target_pairs={{1,0},{2,1},{3,2},{4,3},{5,4},{6,5},{7,6},{8,7},{9,8},{10,9},{11,1... | collective-permute-start | bytes 98312 | tf_op jit(solution)/shard_map/ppermute | solution.py:24
  196.3 6.2 %collective-permute-start.6 = (f32[1,1,64,128]{2,3,1,0:T(8,128)S(1)}, f32[1,1,64,128]{2,3,1,0:T(8,128)S(1)}, u32[]{:S(2)}, u32[]{:S(2)}) collective-permute-start(f32[1,1,64,128]{2,3,1,0:T(8,128)S(1)} %get-tuple-element.249), channel_id=1, source_target_pairs={{0,1},{1,2},{2,3},{3,4},{4,5},{5,6},{6,7},{7,8},{8,9},{9,10},{10,1... | collective-permute-start | bytes 98312 | tf_op jit(solution)/shard_map/ppermute | solution.py:23
  198.2 9.5 %collective-permute-start.7 = (f32[1,1,64,128]{2,3,1,0:T(8,128)S(1)}, f32[1,1,64,128]{2,3,1,0:T(8,128)S(1)}, u32[]{:S(2)}, u32[]{:S(2)}) collective-permute-start(f32[1,1,64,128]{2,3,1,0:T(8,128)S(1)} %get-tuple-element.250), channel_id=1, source_target_pairs={{1,0},{2,1},{3,2},{4,3},{5,4},{6,5},{7,6},{8,7},{9,8},{10,9},{11,1... | collective-permute-start | bytes 98312 | tf_op jit(solution)/shard_map/ppermute | solution.py:24
  222.0 73.8 %copy-start.5 = (f32[2,32,64]{2,1,0:T(8,128)}, f32[2,32,64]{2,1,0:T(8,128)S(1)}, u32[]{:S(2)}) copy-start(f32[2,32,64]{2,1,0:T(8,128)S(1)} %reduce_sum.75) | copy-start | bytes 49156
  222.1 22.1 %copy-start.15 = (f32[1,1,32,64]{3,2,1,0:T(8,128)}, f32[1,1,32,64]{3,2,1,0:T(8,128)S(1)}, u32[]{:S(2)}) copy-start(f32[1,1,32,64]{3,2,1,0:T(8,128)S(1)} %collective-permute-done.4) | copy-start | bytes 24580
  222.1 22.1 %copy-start.16 = (f32[1,1,32,64]{3,2,1,0:T(8,128)}, f32[1,1,32,64]{3,2,1,0:T(8,128)S(1)}, u32[]{:S(2)}) copy-start(f32[1,1,32,64]{3,2,1,0:T(8,128)S(1)} %collective-permute-done.5) | copy-start | bytes 24580
  222.3 5.9 %collective-permute-start.8 = (f32[1,1,32,64]{3,2,1,0:T(8,128)S(1)}, f32[1,1,32,64]{3,2,1,0:T(8,128)S(1)}, u32[]{:S(2)}, u32[]{:S(2)}) collective-permute-start(f32[1,1,32,64]{3,2,1,0:T(8,128)S(1)} %get-tuple-element.293), channel_id=1, source_target_pairs={{0,1},{1,2},{2,3},{3,4},{4,5},{5,6},{6,7},{7,8},{8,9},{9,10},{10,1... | collective-permute-start | bytes 24584 | tf_op jit(solution)/shard_map/ppermute | solution.py:23
  224.2 9.0 %collective-permute-start.9 = (f32[1,1,32,64]{3,2,1,0:T(8,128)S(1)}, f32[1,1,32,64]{3,2,1,0:T(8,128)S(1)}, u32[]{:S(2)}, u32[]{:S(2)}) collective-permute-start(f32[1,1,32,64]{3,2,1,0:T(8,128)S(1)} %get-tuple-element.294), channel_id=1, source_target_pairs={{1,0},{2,1},{3,2},{4,3},{5,4},{6,5},{7,6},{8,7},{9,8},{10,9},{11,1... | collective-permute-start | bytes 24584 | tf_op jit(solution)/shard_map/ppermute | solution.py:24
  233.3 5.9 %collective-permute-start.10 = (f32[1,1,32,64]{3,2,1,0:T(8,128)S(1)}, f32[1,1,32,64]{3,2,1,0:T(8,128)S(1)}, u32[]{:S(2)}, u32[]{:S(2)}) collective-permute-start(f32[1,1,32,64]{3,2,1,0:T(8,128)S(1)} %get-tuple-element.287), channel_id=1, source_target_pairs={{0,1},{1,2},{2,3},{3,4},{4,5},{5,6},{6,7},{7,8},{8,9},{9,10},{10,1... | collective-permute-start | bytes 24584 | tf_op jit(solution)/shard_map/ppermute | solution.py:23
  235.2 9.0 %collective-permute-start.11 = (f32[1,1,32,64]{3,2,1,0:T(8,128)S(1)}, f32[1,1,32,64]{3,2,1,0:T(8,128)S(1)}, u32[]{:S(2)}, u32[]{:S(2)}) collective-permute-start(f32[1,1,32,64]{3,2,1,0:T(8,128)S(1)} %get-tuple-element.288), channel_id=1, source_target_pairs={{1,0},{2,1},{3,2},{4,3},{5,4},{6,5},{7,6},{8,7},{9,8},{10,9},{11,1... | collective-permute-start | bytes 24584 | tf_op jit(solution)/shard_map/ppermute | solution.py:24
  397.3 41.0 %copy-start.2 = (f32[1,1,64,128]{2,3,1,0:T(8,128)S(1)}, f32[1,1,64,128]{2,3,1,0:T(8,128)}, u32[]{:S(2)}) copy-start(f32[1,1,64,128]{2,3,1,0:T(8,128)} %copy-done.1) | copy-start | bytes 98308
  397.3 41.0 %copy-start.4 = (f32[1,1,64,128]{2,3,1,0:T(8,128)S(1)}, f32[1,1,64,128]{2,3,1,0:T(8,128)}, u32[]{:S(2)}) copy-start(f32[1,1,64,128]{2,3,1,0:T(8,128)} %copy-done.3) | copy-start | bytes 98308
  400.2 6.6 %collective-permute-start.12 = (f32[1,1,32,64]{3,2,1,0:T(8,128)S(1)}, f32[1,1,32,64]{3,2,1,0:T(8,128)S(1)}, u32[]{:S(2)}, u32[]{:S(2)}) collective-permute-start(f32[1,1,32,64]{3,2,1,0:T(8,128)S(1)} %get-tuple-element.279), channel_id=1, source_target_pairs={{0,1},{1,2},{2,3},{3,4},{4,5},{5,6},{6,7},{7,8},{8,9},{9,10},{10,1... | collective-permute-start | bytes 24584 | tf_op jit(solution)/shard_map/ppermute | solution.py:23
  404.8 9.0 %collective-permute-start.13 = (f32[1,1,32,64]{3,2,1,0:T(8,128)S(1)}, f32[1,1,32,64]{3,2,1,0:T(8,128)S(1)}, u32[]{:S(2)}, u32[]{:S(2)}) collective-permute-start(f32[1,1,32,64]{3,2,1,0:T(8,128)S(1)} %get-tuple-element.280), channel_id=1, source_target_pairs={{1,0},{2,1},{3,2},{4,3},{5,4},{6,5},{7,6},{8,7},{9,8},{10,9},{11,1... | collective-permute-start | bytes 24584 | tf_op jit(solution)/shard_map/ppermute | solution.py:24
  414.7 5.9 %collective-permute-start.14 = (f32[1,1,32,64]{3,2,1,0:T(8,128)S(1)}, f32[1,1,32,64]{3,2,1,0:T(8,128)S(1)}, u32[]{:S(2)}, u32[]{:S(2)}) collective-permute-start(f32[1,1,32,64]{3,2,1,0:T(8,128)S(1)} %get-tuple-element.273), channel_id=1, source_target_pairs={{0,1},{1,2},{2,3},{3,4},{4,5},{5,6},{6,7},{7,8},{8,9},{9,10},{10,1... | collective-permute-start | bytes 24584 | tf_op jit(solution)/shard_map/ppermute | solution.py:23
  416.7 9.0 %collective-permute-start.15 = (f32[1,1,32,64]{3,2,1,0:T(8,128)S(1)}, f32[1,1,32,64]{3,2,1,0:T(8,128)S(1)}, u32[]{:S(2)}, u32[]{:S(2)}) collective-permute-start(f32[1,1,32,64]{3,2,1,0:T(8,128)S(1)} %get-tuple-element.274), channel_id=1, source_target_pairs={{1,0},{2,1},{3,2},{4,3},{5,4},{6,5},{7,6},{8,7},{9,8},{10,9},{11,1... | collective-permute-start | bytes 24584 | tf_op jit(solution)/shard_map/ppermute | solution.py:24
  426.9 6.2 %collective-permute-start.16 = (f32[1,1,64,128]{2,3,1,0:T(8,128)S(1)}, f32[1,1,64,128]{2,3,1,0:T(8,128)S(1)}, u32[]{:S(2)}, u32[]{:S(2)}) collective-permute-start(f32[1,1,64,128]{2,3,1,0:T(8,128)S(1)} %get-tuple-element.219), channel_id=1, source_target_pairs={{0,1},{1,2},{2,3},{3,4},{4,5},{5,6},{6,7},{7,8},{8,9},{9,10},{10,1... | collective-permute-start | bytes 98312 | tf_op jit(solution)/shard_map/ppermute | solution.py:23
  428.8 9.5 %collective-permute-start.17 = (f32[1,1,64,128]{2,3,1,0:T(8,128)S(1)}, f32[1,1,64,128]{2,3,1,0:T(8,128)S(1)}, u32[]{:S(2)}, u32[]{:S(2)}) collective-permute-start(f32[1,1,64,128]{2,3,1,0:T(8,128)S(1)} %get-tuple-element.220), channel_id=1, source_target_pairs={{1,0},{2,1},{3,2},{4,3},{5,4},{6,5},{7,6},{8,7},{9,8},{10,9},{11,1... | collective-permute-start | bytes 98312 | tf_op jit(solution)/shard_map/ppermute | solution.py:24
  439.6 6.2 %collective-permute-start.18 = (f32[1,1,64,128]{2,3,1,0:T(8,128)S(1)}, f32[1,1,64,128]{2,3,1,0:T(8,128)S(1)}, u32[]{:S(2)}, u32[]{:S(2)}) collective-permute-start(f32[1,1,64,128]{2,3,1,0:T(8,128)S(1)} %get-tuple-element.213), channel_id=1, source_target_pairs={{0,1},{1,2},{2,3},{3,4},{4,5},{5,6},{6,7},{7,8},{8,9},{9,10},{10,1... | collective-permute-start | bytes 98312 | tf_op jit(solution)/shard_map/ppermute | solution.py:23
  441.5 9.5 %collective-permute-start.19 = (f32[1,1,64,128]{2,3,1,0:T(8,128)S(1)}, f32[1,1,64,128]{2,3,1,0:T(8,128)S(1)}, u32[]{:S(2)}, u32[]{:S(2)}) collective-permute-start(f32[1,1,64,128]{2,3,1,0:T(8,128)S(1)} %get-tuple-element.214), channel_id=1, source_target_pairs={{1,0},{2,1},{3,2},{4,3},{5,4},{6,5},{7,6},{8,7},{9,8},{10,9},{11,1... | collective-permute-start | bytes 98312 | tf_op jit(solution)/shard_map/ppermute | solution.py:24
  (11 other events, 156.1 us)
Sparse Core Ops, SparseCore 0:
  9.7 66.4 all-reduce.60
where the time goes:
time: 465 us; the launch traced here: 460 us
  waiting for transfers between devices  111 us (24%)
  other arithmetic  108 us (23%)
  blocking collectives  94.6 us (20%)
  starting transfers between devices  66.4 us (14%)
  local copies, waits for them, and re-layouts  62.8 us (14%)
  between operations  15 us (3%)
    add x71, other arithmetic, sweep(): return values + coefs[7] * (right - apply_op(values, pad_z(values), coefs))  82.6 us
    psum x1, waiting for transfers between devices, from_root(): return lax.psum(jnp.where(mine, x, jnp.zeros_like(x)), axis)  65.1 us
    all_gather x1, blocking collectives, spread_cycle(): lax.all_gather(field, 'dom', axis=1, tiled=True)  48.6 us
    all_gather x1, blocking collectives, spread_cycle(): lax.all_gather(right_side, 'dom', axis=1, tiled=True)  46 us
    ppermute x10, waiting for transfers between devices, padded_2(): after = lax.ppermute(initial, axis, down)  45.1 us
    ppermute x10, starting transfers between devices, padded_2(): before = lax.ppermute(last, axis, up)  35.2 us
    ppermute x10, starting transfers between devices, padded_2(): after = lax.ppermute(initial, axis, down)  31.2 us
    reshape x4, local copies, waits for them, and re-layouts, sum_children(): values.reshape(shape[:-3] + (shape[-3] // 2, 2, shape[-2] // 2, 2, shape[...  29.6 us
  transfers between devices with their start and end apart: 21, of which 12 were waited for; matrix products, arithmetic and copies ran while one was open for 6% of the time, Pallas kernels for 0%

commit v1 on v0

--- a/solution.py
+++ b/solution.py
@@ -28,7 +28,7 @@
 
 def from_root(x, axis, root):
     mine = lax.axis_index(axis) == root
-    return lax.psum(jnp.where(mine, x, jnp.zeros_like(x)), axis)
+    return jnp.sum(lax.all_gather(jnp.where(mine, x, jnp.zeros_like(x)), axis_name=axis), axis=0)
 
 
 def shift_lower(values, axis):

time: 465 us -> 390 us (0.84)
  waiting for transfers between devices: 111 us -> 73.1 us
  other arithmetic: 108 us -> 86.9 us
  local copies, waits for them, and re-layouts: 62.8 us -> 47.3 us
    psum x1 -> x0, waiting for transfers between devices: 65.1 us -> none  [from_root(): return lax.psum(jnp.where(mine, x, jnp.zeros_like(x)), axis)]
    all_gather x0 -> x1, waiting for transfers between devices: none -> 28.9 us  [from_root(): lax.all_gather(jnp.where(mine, x, jnp.zeros_like(x)), axis_name=axis)]
    add x71, other arithmetic: 82.6 us -> 63.1 us  [sweep(): return values + coefs[7] * (right - apply_op(values, pad_z(values), coefs))]
    while x10, local copies, waits for them, and re-layouts: 10.3 us -> 3.56 us  [coarse_solve(): lax.fori_loop(0, COARSE_SWEEPS - 1, lambda step, values: sweep(values, ri...]
  transfers between devices with their start and end apart: 21 -> 21, of which waited for: 12 -> 9; matrix products, arithmetic and copies ran while one was open for 6% -> 4% of each run, Pallas kernels for 0% -> 0%
where the time goes in v1:
time: 390 us; the launch traced here: 386 us
  blocking collectives  94.7 us (24%)
  other arithmetic  86.9 us (22%)
  waiting for transfers between devices  73.1 us (19%)
  starting transfers between devices  66.4 us (17%)
  local copies, waits for them, and re-layouts  47.3 us (12%)
  between operations  15.2 us (4%)
    add x71, other arithmetic, sweep(): return values + coefs[7] * (right - apply_op(values, pad_z(values), coefs))  63.1 us
    all_gather x1, blocking collectives, spread_cycle(): lax.all_gather(field, 'dom', axis=1, tiled=True)  48.7 us
    all_gather x1, blocking collectives, spread_cycle(): lax.all_gather(right_side, 'dom', axis=1, tiled=True)  46 us
    ppermute x10, waiting for transfers between devices, padded_2(): after = lax.ppermute(initial, axis, down)  44.2 us
    ppermute x10, starting transfers between devices, padded_2(): before = lax.ppermute(last, axis, up)  35.2 us
    ppermute x10, starting transfers between devices, padded_2(): after = lax.ppermute(initial, axis, down)  31.2 us
    reshape x4, local copies, waits for them, and re-layouts, sum_children(): values.reshape(shape[:-3] + (shape[-3] // 2, 2, shape[-2] // 2, 2, shape[...  29.6 us
    all_gather x1, waiting for transfers between devices, from_root(): lax.all_gather(jnp.where(mine, x, jnp.zeros_like(x)), axis_name=axis)  28.9 us
  transfers between devices with their start and end apart: 21, of which 9 were waited for; matrix products, arithmetic and copies ran while one was open for 4% of the time, Pallas kernels for 0%

profile of v1, /device:TPU:120, one launch (start us, length us, event | category | flops | bytes accessed | tf_op | source)
XLA Modules:
  0.0 385.6 jit_solution(14852028093009958316)
XLA Ops:
  7.9 28.9 %all-gather.4.cloned.1.call-done = f32[8,4,64,128]{3,2,1,0:T(8,128)} async-done(((f32[1,4,64,128]{3,2,1,0:T(8,128)}), f32[8,4,64,128]{3,2,1,0:T(8,128)}) %all-gather.4.cloned.1.call-update) | async-done | bytes 1048592 | tf_op jit(solution)/shard_map/all_gather | solution.py:31
  39.3 9.8 %reshape.773 = f32[2,2,32,2,64,2]{5,4,3,2,1,0:T(8,128)} reshape(f32[1,4,64,128]{3,2,1,0:T(8,128)S(1)} %fusion.63) | data formatting | bytes 262144 | tf_op jit(solution)/shard_map/reshape | solution.py:92
  49.1 4.0 %reduce_sum.84 = f32[2,32,64]{2,1,0:T(8,128)S(1)} reduce(f32[2,2,32,2,64,2]{5,4,3,2,1,0:T(8,128)} %reshape.773, f32[]{:T(128)} %constant.37.clone.1), dimensions={1,3,5}, to_apply=%region_1.2 | reduce | flops 28672 | bytes 147460 | tf_op jit(solution)/shard_map/reduce_sum | solution.py:93
  54.1 48.7 %all-gather = f32[512,32]{1,0:T(8,128)S(1)} all-gather(f32[16,32]{1,0:T(8,128)S(1)} %broadcast_multiply_fusion), channel_id=2, replica_groups=mesh['prop'=8,'dom'=32] {'dom'}, dimensions={0}, use_global_device_ids=true | all-gather | bytes 67584 | tf_op jit(solution)/shard_map/all_gather | solution.py:154
  105.4 5.5 %reshape.775 = f32[16,2,8,2,16,2]{3,2,1,0,5,4:T(8,128)} reshape(f32[512,32]{0,1:T(8,128)S(1)} %copy.40) | data formatting | bytes 131072 | tf_op jit(solution)/shard_map/reshape | solution.py:92
  110.9 2.6 reduce_sum.94
  113.7 4.6 %collective-permute-start = (f32[1,1,64,128]{3,2,1,0:T(8,128)S(1)}, f32[1,1,64,128]{3,2,1,0:T(8,128)S(1)}, u32[]{:S(2)}, u32[]{:S(2)}) collective-permute-start(f32[1,1,64,128]{3,2,1,0:T(8,128)S(1)} %get-tuple-element.266), channel_id=1, source_target_pairs={{0,1},{1,2},{2,3},{3,4},{4,5},{5,6},{6,7},{7,8},{8,9},{9,10},{10,1... | collective-permute-start | bytes 98312 | tf_op jit(solution)/shard_map/ppermute | solution.py:23
  118.3 1.9 collective-permute-start.1
  120.3 7.2 %collective-permute-start.4 = (f32[1,1,32,64]{3,2,1,0:T(8,128)S(1)}, f32[1,1,32,64]{3,2,1,0:T(8,128)S(1)}, u32[]{:S(2)}, u32[]{:S(2)}) collective-permute-start(f32[1,1,32,64]{3,2,1,0:T(8,128)S(1)} %get-tuple-element.298), channel_id=1, source_target_pairs={{0,1},{1,2},{2,3},{3,4},{4,5},{5,6},{6,7},{7,8},{8,9},{9,10},{10,1... | collective-permute-start | bytes 24584 | tf_op jit(solution)/shard_map/ppermute | solution.py:23
  130.8 7.2 %collective-permute-start.2 = (f32[1,1,64,128]{3,2,1,0:T(8,128)S(1)}, f32[1,1,64,128]{3,2,1,0:T(8,128)S(1)}, u32[]{:S(2)}, u32[]{:S(2)}) collective-permute-start(f32[1,1,64,128]{3,2,1,0:T(8,128)S(1)} %get-tuple-element.261), channel_id=1, source_target_pairs={{0,1},{1,2},{2,3},{3,4},{4,5},{5,6},{6,7},{7,8},{8,9},{9,10},{10,1... | collective-permute-start | bytes 98312 | tf_op jit(solution)/shard_map/ppermute | solution.py:23
  140.1 7.1 %collective-permute-done.3 = f32[1,1,64,128]{3,2,1,0:T(8,128)S(1)} collective-permute-done((f32[1,1,64,128]{3,2,1,0:T(8,128)S(1)}, f32[1,1,64,128]{3,2,1,0:T(8,128)S(1)}, u32[]{:S(2)}, u32[]{:S(2)}) %collective-permute-start.3) | collective-permute-done | bytes 32800 | tf_op jit(solution)/shard_map/ppermute | solution.py:24
  149.3 3.9 %collective-permute-start.7 = (f32[1,1,64,128]{3,2,1,0:T(8,128)S(1)}, f32[1,1,64,128]{3,2,1,0:T(8,128)S(1)}, u32[]{:S(2)}, u32[]{:S(2)}) collective-permute-start(f32[1,1,64,128]{3,2,1,0:T(8,128)S(1)} %get-tuple-element.256), channel_id=1, source_target_pairs={{1,0},{2,1},{3,2},{4,3},{5,4},{6,5},{7,6},{8,7},{9,8},{10,9},{11,1... | collective-permute-start | bytes 98312 | tf_op jit(solution)/shard_map/ppermute | solution.py:24
  153.4 5.1 %collective-permute-done.7 = f32[1,1,64,128]{3,2,1,0:T(8,128)S(1)} collective-permute-done((f32[1,1,64,128]{3,2,1,0:T(8,128)S(1)}, f32[1,1,64,128]{3,2,1,0:T(8,128)S(1)}, u32[]{:S(2)}, u32[]{:S(2)}) %collective-permute-start.7) | collective-permute-done | bytes 32800 | tf_op jit(solution)/shard_map/ppermute | solution.py:24
  158.7 9.8 %reshape.774 = f32[2,2,32,2,64,2]{5,4,3,2,1,0:T(8,128)} reshape(f32[1,4,64,128]{3,2,1,0:T(8,128)S(1)} %fusion.43) | data formatting | bytes 262144 | tf_op jit(solution)/shard_map/reshape | solution.py:92
  168.5 4.0 %reduce_sum.85 = f32[2,32,64]{2,1,0:T(8,128)S(1)} reduce(f32[2,2,32,2,64,2]{5,4,3,2,1,0:T(8,128)} %reshape.774, f32[]{:T(128)} %constant.37.clone.1), dimensions={1,3,5}, to_apply=%region_2.3 | reduce | flops 28672 | bytes 147460 | tf_op jit(solution)/shard_map/reduce_sum | solution.py:93
  174.6 3.9 %collective-permute-start.9 = (f32[1,1,32,64]{3,2,1,0:T(8,128)S(1)}, f32[1,1,32,64]{3,2,1,0:T(8,128)S(1)}, u32[]{:S(2)}, u32[]{:S(2)}) collective-permute-start(f32[1,1,32,64]{3,2,1,0:T(8,128)S(1)} %get-tuple-element.294), channel_id=1, source_target_pairs={{1,0},{2,1},{3,2},{4,3},{5,4},{6,5},{7,6},{8,7},{9,8},{10,9},{11,1... | collective-permute-start | bytes 24584 | tf_op jit(solution)/shard_map/ppermute | solution.py:24
  178.6 4.9 %collective-permute-done.9 = f32[1,1,32,64]{3,2,1,0:T(8,128)S(1)} collective-permute-done((f32[1,1,32,64]{3,2,1,0:T(8,128)S(1)}, f32[1,1,32,64]{3,2,1,0:T(8,128)S(1)}, u32[]{:S(2)}, u32[]{:S(2)}) %collective-permute-start.9) | collective-permute-done | bytes 8224 | tf_op jit(solution)/shard_map/ppermute | solution.py:24
  183.7 1.9 collective-permute-start.10
  185.6 3.9 %collective-permute-start.11 = (f32[1,1,32,64]{3,2,1,0:T(8,128)S(1)}, f32[1,1,32,64]{3,2,1,0:T(8,128)S(1)}, u32[]{:S(2)}, u32[]{:S(2)}) collective-permute-start(f32[1,1,32,64]{3,2,1,0:T(8,128)S(1)} %get-tuple-element.288), channel_id=1, source_target_pairs={{1,0},{2,1},{3,2},{4,3},{5,4},{6,5},{7,6},{8,7},{9,8},{10,9},{11,1... | collective-permute-start | bytes 24584 | tf_op jit(solution)/shard_map/ppermute | solution.py:24
  189.6 4.9 %collective-permute-done.11 = f32[1,1,32,64]{3,2,1,0:T(8,128)S(1)} collective-permute-done((f32[1,1,32,64]{3,2,1,0:T(8,128)S(1)}, f32[1,1,32,64]{3,2,1,0:T(8,128)S(1)}, u32[]{:S(2)}, u32[]{:S(2)}) %collective-permute-start.11) | collective-permute-done | bytes 8224 | tf_op jit(solution)/shard_map/ppermute | solution.py:24
  195.4 46.0 %all-gather.1 = f32[512,32]{1,0:T(8,128)S(1)} all-gather(f32[16,32]{1,0:T(8,128)S(1)} %reduce_sum.92), channel_id=3, replica_groups=mesh['prop'=8,'dom'=32] {'dom'}, dimensions={0}, use_global_device_ids=true | all-gather | bytes 67584 | tf_op jit(solution)/shard_map/all_gather | solution.py:153
  246.3 4.5 %reshape.776 = f32[16,2,8,2,16,2]{5,4,3,2,1,0:T(8,128)} reshape(f32[1,32,16,32]{3,2,1,0:T(8,128)} %fusion.17) | data formatting | bytes 131072 | tf_op jit(solution)/shard_map/reshape | solution.py:92
  250.7 2.5 reduce_sum.95
  258.4 67.8 %while.15 = (s32[]{:T(128)}, f32[1,16,8,16]{3,2,1,0:T(8,128)S(1)}, f32[1,16,8,16]{3,2,1,0:T(8,128)S(1)}, f32[1,16,8,16]{3,2,1,0:T(8,128)S(1)}, f32[1,16,8,16]{3,...) while((s32[]{:T(128)}, f32[1,16,8,16]{3,2,1,0:T(8,128)S(1)}, ...), condition=%wide.region_10.11_spmd, body=%wide.region_9.10_spmd.sunk | while | flops 32770 | bytes 195701 | solution.py:116
  330.4 4.6 %collective-permute-start.12 = (f32[1,1,32,64]{3,2,1,0:T(8,128)S(1)}, f32[1,1,32,64]{3,2,1,0:T(8,128)S(1)}, u32[]{:S(2)}, u32[]{:S(2)}) collective-permute-start(f32[1,1,32,64]{3,2,1,0:T(8,128)S(1)} %get-tuple-element.279), channel_id=1, source_target_pairs={{0,1},{1,2},{2,3},{3,4},{4,5},{5,6},{6,7},{7,8},{8,9},{9,10},{10,1... | collective-permute-start | bytes 24584 | tf_op jit(solution)/shard_map/ppermute | solution.py:23
  337.0 7.0 %collective-permute-done.13 = f32[1,1,32,64]{3,2,1,0:T(8,128)S(1)} collective-permute-done((f32[1,1,32,64]{3,2,1,0:T(8,128)S(1)}, f32[1,1,32,64]{3,2,1,0:T(8,128)S(1)}, u32[]{:S(2)}, u32[]{:S(2)}) %collective-permute-start.13) | collective-permute-done | bytes 8224 | tf_op jit(solution)/shard_map/ppermute | solution.py:24
  346.0 3.9 %collective-permute-start.15 = (f32[1,1,32,64]{3,2,1,0:T(8,128)S(1)}, f32[1,1,32,64]{3,2,1,0:T(8,128)S(1)}, u32[]{:S(2)}, u32[]{:S(2)}) collective-permute-start(f32[1,1,32,64]{3,2,1,0:T(8,128)S(1)} %get-tuple-element.274), channel_id=1, source_target_pairs={{1,0},{2,1},{3,2},{4,3},{5,4},{6,5},{7,6},{8,7},{9,8},{10,9},{11,1... | collective-permute-start | bytes 24584 | tf_op jit(solution)/shard_map/ppermute | solution.py:24
  350.1 4.9 %collective-permute-done.15 = f32[1,1,32,64]{3,2,1,0:T(8,128)S(1)} collective-permute-done((f32[1,1,32,64]{3,2,1,0:T(8,128)S(1)}, f32[1,1,32,64]{3,2,1,0:T(8,128)S(1)}, u32[]{:S(2)}, u32[]{:S(2)}) %collective-permute-start.15) | collective-permute-done | bytes 8224 | tf_op jit(solution)/shard_map/ppermute | solution.py:24
  357.5 3.9 %collective-permute-start.17 = (f32[1,1,64,128]{3,2,1,0:T(8,128)S(1)}, f32[1,1,64,128]{3,2,1,0:T(8,128)S(1)}, u32[]{:S(2)}, u32[]{:S(2)}) collective-permute-start(f32[1,1,64,128]{3,2,1,0:T(8,128)S(1)} %get-tuple-element.244), channel_id=1, source_target_pairs={{1,0},{2,1},{3,2},{4,3},{5,4},{6,5},{7,6},{8,7},{9,8},{10,9},{11,1... | collective-permute-start | bytes 98312 | tf_op jit(solution)/shard_map/ppermute | solution.py:24
  361.5 5.1 %collective-permute-done.17 = f32[1,1,64,128]{3,2,1,0:T(8,128)S(1)} collective-permute-done((f32[1,1,64,128]{3,2,1,0:T(8,128)S(1)}, f32[1,1,64,128]{3,2,1,0:T(8,128)S(1)}, u32[]{:S(2)}, u32[]{:S(2)}) %collective-permute-start.17) | collective-permute-done | bytes 32800 | tf_op jit(solution)/shard_map/ppermute | solution.py:24
  368.8 3.9 %collective-permute-start.19 = (f32[1,1,64,128]{3,2,1,0:T(8,128)S(1)}, f32[1,1,64,128]{3,2,1,0:T(8,128)S(1)}, u32[]{:S(2)}, u32[]{:S(2)}) collective-permute-start(f32[1,1,64,128]{3,2,1,0:T(8,128)S(1)} %get-tuple-element.238), channel_id=1, source_target_pairs={{1,0},{2,1},{3,2},{4,3},{5,4},{6,5},{7,6},{8,7},{9,8},{10,9},{11,1... | collective-permute-start | bytes 98312 | tf_op jit(solution)/shard_map/ppermute | solution.py:24
  372.8 5.1 %collective-permute-done.19 = f32[1,1,64,128]{3,2,1,0:T(8,128)S(1)} collective-permute-done((f32[1,1,64,128]{3,2,1,0:T(8,128)S(1)}, f32[1,1,64,128]{3,2,1,0:T(8,128)S(1)}, u32[]{:S(2)}, u32[]{:S(2)}) %collective-permute-start.19) | collective-permute-done | bytes 32800 | tf_op jit(solution)/shard_map/ppermute | solution.py:24
  (435 shorter events, 106.9 us)
Async XLA Ops:
  6.5 30.2 %all-gather.4.cloned.1.call-start = ((), (), s32[]{:S(2)}) async-start(), calls=%async_computation | async-start | bytes 1179648 | tf_op jit(solution)/shard_map/all_gather | solution.py:31
  39.0 119.5 %copy-start.19 = (f32[1,4,1,128]{3,2,1,0:T(1,128)}, f32[1,4,1,128]{3,2,1,0:T(1,128)S(1)}, u32[]{:S(2)}) copy-start(f32[1,4,1,128]{3,2,1,0:T(1,128)S(1)} %get-tuple-element.267) | copy-start | bytes 6148
  39.0 119.5 %copy-start.21 = (f32[1,4,1,128]{3,2,1,0:T(1,128)}, f32[1,4,1,128]{3,2,1,0:T(1,128)S(1)}, u32[]{:S(2)}) copy-start(f32[1,4,1,128]{3,2,1,0:T(1,128)S(1)} %get-tuple-element.268) | copy-start | bytes 6148
  53.2 141.4 %copy-start.23 = (f32[1,2,1,64]{3,2,1,0:T(1,128)}, f32[1,2,1,64]{3,2,1,0:T(1,128)S(1)}, u32[]{:S(2)}) copy-start(f32[1,2,1,64]{3,2,1,0:T(1,128)S(1)} %get-tuple-element.299) | copy-start | bytes 1540
  53.2 141.4 %copy-start.25 = (f32[1,2,1,64]{3,2,1,0:T(1,128)}, f32[1,2,1,64]{3,2,1,0:T(1,128)S(1)}, u32[]{:S(2)}) copy-start(f32[1,2,1,64]{3,2,1,0:T(1,128)S(1)} %get-tuple-element.300) | copy-start | bytes 1540
  53.2 141.4 %copy-start.4 = (f32[1,2,31,64]{3,2,1,0:T(8,128)}, f32[1,2,31,64]{3,2,1,0:T(8,128)S(1)}, u32[]{:S(2)}) copy-start(f32[1,2,31,64]{3,2,1,0:T(8,128)S(1)} %add_divide_fusion.7) | copy-start | bytes 47620
  54.1 76.5 %copy-start = (f32[4,64,128]{2,1,0:T(8,128)S(1)}, f32[4,64,128]{2,1,0:T(8,128)}, u32[]{:S(2)}) copy-start(f32[4,64,128]{2,1,0:T(8,128)} %param.9) | copy-start | bytes 393220
  113.7 16.8 %collective-permute-start = (f32[1,1,64,128]{3,2,1,0:T(8,128)S(1)}, f32[1,1,64,128]{3,2,1,0:T(8,128)S(1)}, u32[]{:S(2)}, u32[]{:S(2)}) collective-permute-start(f32[1,1,64,128]{3,2,1,0:T(8,128)S(1)} %get-tuple-element.266), channel_id=1, source_target_pairs={{0,1},{1,2},{2,3},{3,4},{4,5},{5,6},{6,7},{7,8},{8,9},{9,10},{10,1... | collective-permute-start | bytes 98312 | tf_op jit(solution)/shard_map/ppermute | solution.py:23
  118.3 12.2 %collective-permute-start.1 = (f32[1,1,64,128]{3,2,1,0:T(8,128)S(1)}, f32[1,1,64,128]{3,2,1,0:T(8,128)S(1)}, u32[]{:S(2)}, u32[]{:S(2)}) collective-permute-start(f32[1,1,64,128]{3,2,1,0:T(8,128)S(1)} %get-tuple-element.265), channel_id=1, source_target_pairs={{1,0},{2,1},{3,2},{4,3},{5,4},{6,5},{7,6},{8,7},{9,8},{10,9},{11,1... | collective-permute-start | bytes 98312 | tf_op jit(solution)/shard_map/ppermute | solution.py:24
  120.3 52.3 %collective-permute-start.4 = (f32[1,1,32,64]{3,2,1,0:T(8,128)S(1)}, f32[1,1,32,64]{3,2,1,0:T(8,128)S(1)}, u32[]{:S(2)}, u32[]{:S(2)}) collective-permute-start(f32[1,1,32,64]{3,2,1,0:T(8,128)S(1)} %get-tuple-element.298), channel_id=1, source_target_pairs={{0,1},{1,2},{2,3},{3,4},{4,5},{5,6},{6,7},{7,8},{8,9},{9,10},{10,1... | collective-permute-start | bytes 24584 | tf_op jit(solution)/shard_map/ppermute | solution.py:23
  127.5 45.0 %collective-permute-start.5 = (f32[1,1,32,64]{3,2,1,0:T(8,128)S(1)}, f32[1,1,32,64]{3,2,1,0:T(8,128)S(1)}, u32[]{:S(2)}, u32[]{:S(2)}) collective-permute-start(f32[1,1,32,64]{3,2,1,0:T(8,128)S(1)} %get-tuple-element.297), channel_id=1, source_target_pairs={{1,0},{2,1},{3,2},{4,3},{5,4},{6,5},{7,6},{8,7},{9,8},{10,9},{11,1... | collective-permute-start | bytes 24584 | tf_op jit(solution)/shard_map/ppermute | solution.py:24
  130.8 9.3 %collective-permute-start.2 = (f32[1,1,64,128]{3,2,1,0:T(8,128)S(1)}, f32[1,1,64,128]{3,2,1,0:T(8,128)S(1)}, u32[]{:S(2)}, u32[]{:S(2)}) collective-permute-start(f32[1,1,64,128]{3,2,1,0:T(8,128)S(1)} %get-tuple-element.261), channel_id=1, source_target_pairs={{0,1},{1,2},{2,3},{3,4},{4,5},{5,6},{6,7},{7,8},{8,9},{9,10},{10,1... | collective-permute-start | bytes 98312 | tf_op jit(solution)/shard_map/ppermute | solution.py:23
  138.0 9.1 %collective-permute-start.3 = (f32[1,1,64,128]{3,2,1,0:T(8,128)S(1)}, f32[1,1,64,128]{3,2,1,0:T(8,128)S(1)}, u32[]{:S(2)}, u32[]{:S(2)}) collective-permute-start(f32[1,1,64,128]{3,2,1,0:T(8,128)S(1)} %get-tuple-element.262), channel_id=1, source_target_pairs={{1,0},{2,1},{3,2},{4,3},{5,4},{6,5},{7,6},{8,7},{9,8},{10,9},{11,1... | collective-permute-start | bytes 98312 | tf_op jit(solution)/shard_map/ppermute | solution.py:24
  147.4 6.0 %collective-permute-start.6 = (f32[1,1,64,128]{3,2,1,0:T(8,128)S(1)}, f32[1,1,64,128]{3,2,1,0:T(8,128)S(1)}, u32[]{:S(2)}, u32[]{:S(2)}) collective-permute-start(f32[1,1,64,128]{3,2,1,0:T(8,128)S(1)} %get-tuple-element.255), channel_id=1, source_target_pairs={{0,1},{1,2},{2,3},{3,4},{4,5},{5,6},{6,7},{7,8},{8,9},{9,10},{10,1... | collective-permute-start | bytes 98312 | tf_op jit(solution)/shard_map/ppermute | solution.py:23
  149.3 9.1 %collective-permute-start.7 = (f32[1,1,64,128]{3,2,1,0:T(8,128)S(1)}, f32[1,1,64,128]{3,2,1,0:T(8,128)S(1)}, u32[]{:S(2)}, u32[]{:S(2)}) collective-permute-start(f32[1,1,64,128]{3,2,1,0:T(8,128)S(1)} %get-tuple-element.256), channel_id=1, source_target_pairs={{1,0},{2,1},{3,2},{4,3},{5,4},{6,5},{7,6},{8,7},{9,8},{10,9},{11,1... | collective-permute-start | bytes 98312 | tf_op jit(solution)/shard_map/ppermute | solution.py:24
  172.5 73.8 %copy-start.1 = (f32[2,32,64]{2,1,0:T(8,128)}, f32[2,32,64]{2,1,0:T(8,128)S(1)}, u32[]{:S(2)}) copy-start(f32[2,32,64]{2,1,0:T(8,128)S(1)} %reduce_sum.85) | copy-start | bytes 49156
  172.5 68.9 %copy-start.15 = (f32[1,1,32,64]{3,2,1,0:T(8,128)}, f32[1,1,32,64]{3,2,1,0:T(8,128)S(1)}, u32[]{:S(2)}) copy-start(f32[1,1,32,64]{3,2,1,0:T(8,128)S(1)} %collective-permute-done.4) | copy-start | bytes 24580
  172.5 68.9 %copy-start.17 = (f32[1,1,32,64]{3,2,1,0:T(8,128)}, f32[1,1,32,64]{3,2,1,0:T(8,128)S(1)}, u32[]{:S(2)}) copy-start(f32[1,1,32,64]{3,2,1,0:T(8,128)S(1)} %collective-permute-done.5) | copy-start | bytes 24580
  172.7 68.8 %copy-start.10 = (f32[1,2,32,64]{3,2,1,0:T(8,128)}, f32[1,2,32,64]{3,2,1,0:T(8,128)S(1)}, u32[]{:S(2)}) copy-start(f32[1,2,32,64]{3,2,1,0:T(8,128)S(1)} %get-tuple-element.200) | copy-start | bytes 49156
  172.7 68.8 %copy-start.12 = (f32[1,2,32,64]{3,2,1,0:T(8,128)}, f32[1,2,32,64]{3,2,1,0:T(8,128)S(1)}, u32[]{:S(2)}) copy-start(f32[1,2,32,64]{3,2,1,0:T(8,128)S(1)} %get-tuple-element.201) | copy-start | bytes 49156
  172.7 5.9 %collective-permute-start.8 = (f32[1,1,32,64]{3,2,1,0:T(8,128)S(1)}, f32[1,1,32,64]{3,2,1,0:T(8,128)S(1)}, u32[]{:S(2)}, u32[]{:S(2)}) collective-permute-start(f32[1,1,32,64]{3,2,1,0:T(8,128)S(1)} %get-tuple-element.293), channel_id=1, source_target_pairs={{0,1},{1,2},{2,3},{3,4},{4,5},{5,6},{6,7},{7,8},{8,9},{9,10},{10,1... | collective-permute-start | bytes 24584 | tf_op jit(solution)/shard_map/ppermute | solution.py:23
  174.6 9.0 %collective-permute-start.9 = (f32[1,1,32,64]{3,2,1,0:T(8,128)S(1)}, f32[1,1,32,64]{3,2,1,0:T(8,128)S(1)}, u32[]{:S(2)}, u32[]{:S(2)}) collective-permute-start(f32[1,1,32,64]{3,2,1,0:T(8,128)S(1)} %get-tuple-element.294), channel_id=1, source_target_pairs={{1,0},{2,1},{3,2},{4,3},{5,4},{6,5},{7,6},{8,7},{9,8},{10,9},{11,1... | collective-permute-start | bytes 24584 | tf_op jit(solution)/shard_map/ppermute | solution.py:24
  183.7 5.9 %collective-permute-start.10 = (f32[1,1,32,64]{3,2,1,0:T(8,128)S(1)}, f32[1,1,32,64]{3,2,1,0:T(8,128)S(1)}, u32[]{:S(2)}, u32[]{:S(2)}) collective-permute-start(f32[1,1,32,64]{3,2,1,0:T(8,128)S(1)} %get-tuple-element.287), channel_id=1, source_target_pairs={{0,1},{1,2},{2,3},{3,4},{4,5},{5,6},{6,7},{7,8},{8,9},{9,10},{10,1... | collective-permute-start | bytes 24584 | tf_op jit(solution)/shard_map/ppermute | solution.py:23
  185.6 9.0 %collective-permute-start.11 = (f32[1,1,32,64]{3,2,1,0:T(8,128)S(1)}, f32[1,1,32,64]{3,2,1,0:T(8,128)S(1)}, u32[]{:S(2)}, u32[]{:S(2)}) collective-permute-start(f32[1,1,32,64]{3,2,1,0:T(8,128)S(1)} %get-tuple-element.288), channel_id=1, source_target_pairs={{1,0},{2,1},{3,2},{4,3},{5,4},{6,5},{7,6},{8,7},{9,8},{10,9},{11,1... | collective-permute-start | bytes 24584 | tf_op jit(solution)/shard_map/ppermute | solution.py:24
  330.4 6.6 %collective-permute-start.12 = (f32[1,1,32,64]{3,2,1,0:T(8,128)S(1)}, f32[1,1,32,64]{3,2,1,0:T(8,128)S(1)}, u32[]{:S(2)}, u32[]{:S(2)}) collective-permute-start(f32[1,1,32,64]{3,2,1,0:T(8,128)S(1)} %get-tuple-element.279), channel_id=1, source_target_pairs={{0,1},{1,2},{2,3},{3,4},{4,5},{5,6},{6,7},{7,8},{8,9},{9,10},{10,1... | collective-permute-start | bytes 24584 | tf_op jit(solution)/shard_map/ppermute | solution.py:23
  335.0 9.0 %collective-permute-start.13 = (f32[1,1,32,64]{3,2,1,0:T(8,128)S(1)}, f32[1,1,32,64]{3,2,1,0:T(8,128)S(1)}, u32[]{:S(2)}, u32[]{:S(2)}) collective-permute-start(f32[1,1,32,64]{3,2,1,0:T(8,128)S(1)} %get-tuple-element.280), channel_id=1, source_target_pairs={{1,0},{2,1},{3,2},{4,3},{5,4},{6,5},{7,6},{8,7},{9,8},{10,9},{11,1... | collective-permute-start | bytes 24584 | tf_op jit(solution)/shard_map/ppermute | solution.py:24
  344.1 5.9 %collective-permute-start.14 = (f32[1,1,32,64]{3,2,1,0:T(8,128)S(1)}, f32[1,1,32,64]{3,2,1,0:T(8,128)S(1)}, u32[]{:S(2)}, u32[]{:S(2)}) collective-permute-start(f32[1,1,32,64]{3,2,1,0:T(8,128)S(1)} %get-tuple-element.273), channel_id=1, source_target_pairs={{0,1},{1,2},{2,3},{3,4},{4,5},{5,6},{6,7},{7,8},{8,9},{9,10},{10,1... | collective-permute-start | bytes 24584 | tf_op jit(solution)/shard_map/ppermute | solution.py:23
  346.0 9.0 %collective-permute-start.15 = (f32[1,1,32,64]{3,2,1,0:T(8,128)S(1)}, f32[1,1,32,64]{3,2,1,0:T(8,128)S(1)}, u32[]{:S(2)}, u32[]{:S(2)}) collective-permute-start(f32[1,1,32,64]{3,2,1,0:T(8,128)S(1)} %get-tuple-element.274), channel_id=1, source_target_pairs={{1,0},{2,1},{3,2},{4,3},{5,4},{6,5},{7,6},{8,7},{9,8},{10,9},{11,1... | collective-permute-start | bytes 24584 | tf_op jit(solution)/shard_map/ppermute | solution.py:24
  355.5 6.0 %collective-permute-start.16 = (f32[1,1,64,128]{3,2,1,0:T(8,128)S(1)}, f32[1,1,64,128]{3,2,1,0:T(8,128)S(1)}, u32[]{:S(2)}, u32[]{:S(2)}) collective-permute-start(f32[1,1,64,128]{3,2,1,0:T(8,128)S(1)} %get-tuple-element.243), channel_id=1, source_target_pairs={{0,1},{1,2},{2,3},{3,4},{4,5},{5,6},{6,7},{7,8},{8,9},{9,10},{10,1... | collective-permute-start | bytes 98312 | tf_op jit(solution)/shard_map/ppermute | solution.py:23
  357.5 9.1 %collective-permute-start.17 = (f32[1,1,64,128]{3,2,1,0:T(8,128)S(1)}, f32[1,1,64,128]{3,2,1,0:T(8,128)S(1)}, u32[]{:S(2)}, u32[]{:S(2)}) collective-permute-start(f32[1,1,64,128]{3,2,1,0:T(8,128)S(1)} %get-tuple-element.244), channel_id=1, source_target_pairs={{1,0},{2,1},{3,2},{4,3},{5,4},{6,5},{7,6},{8,7},{9,8},{10,9},{11,1... | collective-permute-start | bytes 98312 | tf_op jit(solution)/shard_map/ppermute | solution.py:24
  366.9 6.0 %collective-permute-start.18 = (f32[1,1,64,128]{3,2,1,0:T(8,128)S(1)}, f32[1,1,64,128]{3,2,1,0:T(8,128)S(1)}, u32[]{:S(2)}, u32[]{:S(2)}) collective-permute-start(f32[1,1,64,128]{3,2,1,0:T(8,128)S(1)} %get-tuple-element.237), channel_id=1, source_target_pairs={{0,1},{1,2},{2,3},{3,4},{4,5},{5,6},{6,7},{7,8},{8,9},{9,10},{10,1... | collective-permute-start | bytes 98312 | tf_op jit(solution)/shard_map/ppermute | solution.py:23
  368.8 9.1 %collective-permute-start.19 = (f32[1,1,64,128]{3,2,1,0:T(8,128)S(1)}, f32[1,1,64,128]{3,2,1,0:T(8,128)S(1)}, u32[]{:S(2)}, u32[]{:S(2)}) collective-permute-start(f32[1,1,64,128]{3,2,1,0:T(8,128)S(1)} %get-tuple-element.238), channel_id=1, source_target_pairs={{1,0},{2,1},{3,2},{4,3},{5,4},{6,5},{7,6},{8,7},{9,8},{10,9},{11,1... | collective-permute-start | bytes 98312 | tf_op jit(solution)/shard_map/ppermute | solution.py:24
  (16 other events, 370.4 us)
Sparse Core Ops, SparseCore 0:
  9.2 27.4 all-gather.3
